TPU v7x, 32 devices: a whole 2x2x4 slice. The times are simulated.
32 devices in a mesh: gx: 4 (over x, core), gy: 4 (over z), gz: 2 (over y).
Axes of the slice: x: 2, y: 2, z: 4, core: 2. Of those that a mesh axis runs over, the one named last changes fastest.
Arguments:
- positions: float32 [3, 16384], P(None, ('gx', 'gy', 'gz')), may hold values from 0 to 4, as said below
- velocities: float32 [3, 16384], P(None, ('gx', 'gy', 'gz')), may hold values from -3 to 3
- star_mass: float32 [16384], P(('gx', 'gy', 'gz')), may hold values from 0.0009765625 to 0.00390625
- far_previous: float32 [3, 16384], P(None, ('gx', 'gy', 'gz')), may hold values from -6 to 6
- cell_index: int32 [16384], P(('gx', 'gy', 'gz')), may hold values from 0 to 15, as said below
- ghost_list: int32 [8192], P(('gx', 'gy', 'gz')), may hold values from 0 to 511, as said below
- block_index: int32 [512, 128], P(('gx', 'gy', 'gz')), may hold values from 0 to 7423, as said below
- block_owner: int32 [512, 1], P(('gx', 'gy', 'gz')), may hold values from 0 to 1; in each aligned block of 16 rows (0 to 15, 16 to 31, ...) at most 16 rows name the same one
- substeps: int32 [512], P(('gx', 'gy', 'gz')), may hold values from 1 to 8, as said below
Outputs:
- far_acc: float32 [3, 16384], P(None, ('gx', 'gy', 'gz'))
- block_state: float32 [6, 131072], P(None, ('gx', 'gy', 'gz'))
Inputs may be any that keep to these rules, and one draw needn't show every extreme that they name: `positions`: stars of the domain with coordinates (a, b, c) lie inside the unit box whose lowest corner is (a, b, c). `cell_index`: each cell of a domain is a box of a regular split of the domain's box, and holds at least 16 of its stars. `ghost_list`: A domain's 256 entries are distinct. `block_index`: each block's 128 entries are distinct pool columns of stars around one of the domain's own stars; no entry is a column of the domain's own sent stars or of a domain outside the grid. `block_owner`: no more than 16 of one domain's blocks have the same owner; in every draw some domain gives exactly 16 blocks to one owner. Every domain has a block with 8 substeps.
All inputs are finite; a program needn't handle non-finite values.
Results may differ from a plain program's by a relative error of at most 0.0003.
Values sent between devices are 32-bit elements; how exact they have to be, the bound alone decides.
A program may use at most 64 MiB of HBM per device.

v0:
```python
import functools

import jax
import jax.numpy as jnp
from jax import lax
from jax.experimental import pallas as pl
from jax.experimental.pallas import tpu as pltpu
from jax.sharding import PartitionSpec as P

CELLS = 16
BLOCKS_DEV = 16
SUBMAX = 8
AXES = ("gx", "gy", "gz")
MESH = pl.DeviceIdType.MESH
LANES = 128

SOFTENING = 0.0025
INNER_RADIUS = 0.25
OUTER_RADIUS = 1.0
TIME_STEP = 0.25
SPAN = OUTER_RADIUS - INNER_RADIUS

BF16 = jnp.bfloat16
F32 = jnp.float32


def three(value):
    high = value.astype(BF16).astype(F32)
    rest = value - high
    middle = rest.astype(BF16).astype(F32)
    low = (rest - middle).astype(BF16).astype(F32)
    return high, middle, low


def pick(chunks, index):
    index = jnp.broadcast_to(index, (8, LANES))
    lane, chunk = index & (LANES - 1), index >> 7
    found = jnp.zeros((8, LANES), F32)
    for number, piece in chunks:
        found = jnp.where(chunk == number, jnp.take_along_axis(piece, lane, axis=1), found)
    return found


def prepare(pos_ref, vel_ref, mass_ref, far_ref, cell_ref, ghost_ref, rows_ref, sent_ref, moment_ref):
    stars = pos_ref.shape[1]
    position, mass = pos_ref[...], mass_ref[...]
    kicked = vel_ref[...] + far_ref[...] * (0.5 * TIME_STEP)
    rows = jnp.concatenate([position, kicked, mass, jnp.zeros((1, stars), F32)], axis=0)
    chunks = []
    for number in range(stars // LANES):
        piece = rows[:, number * LANES : (number + 1) * LANES]
        rows_ref[number] = piece
        chunks.append((number, piece))
    for number in range(ghost_ref.shape[1] // LANES):
        sent_ref[number] = pick(chunks, ghost_ref[:, number * LANES : (number + 1) * LANES])
    cell = lax.broadcasted_iota(jnp.int32, (LANES, stars), 0)
    member = jnp.where(jnp.broadcast_to(cell_ref[...], (LANES, stars)) == cell, 1.0, 0.0).astype(BF16)
    weighted = jnp.concatenate([mass, position * mass, jnp.zeros((4, stars), F32)], axis=0)
    parts = jnp.concatenate([*three(weighted), jnp.zeros_like(weighted)], axis=0).astype(BF16)
    sums = lax.dot_general(parts, member, (((1,), (1,)), ((), ())), preferred_element_type=F32)
    sums = sums[0:8] + sums[8:16] + sums[16:24]
    inside = lax.broadcasted_iota(jnp.int32, (1, LANES), 1) < CELLS
    total = jnp.where(inside, sums[0:1], 0.0)
    packed = total
    for axis in range(3):
        centre = jnp.where(inside, sums[axis + 1 : axis + 2] / jnp.where(inside, total, 1.0), 0.0)
        packed = packed + pltpu.roll(centre, (axis + 1) * CELLS, 1)
    moment_ref[0] = packed


def exchange(
    sizes, pos_ref, vel_ref, mass_ref, far_ref, cell_ref, ghost_ref, rows_ref, near_ref, every_ref,
    sent_ref, moment_ref, own_sem, moment_sems, send_sems, recv_sems,
):
    count = sizes[0] * sizes[1] * sizes[2]
    here = tuple(lax.axis_index(axis) for axis in AXES)
    barrier = pltpu.get_barrier_semaphore()

    turned = [[lax.rem(at + k, size) for k in range(size)] for at, size in zip(here[:2], sizes)]
    few = sizes[2] <= 4

    def each(act):
        for x, at_x in enumerate(turned[0]):
            for y, at_y in enumerate(turned[1]):
                first = 1 if x == 0 and y == 0 else 0

                def one(z, carry):
                    act((x * sizes[1] + y) * sizes[2] + z, (at_x, at_y, lax.rem(here[2] + z, sizes[2])))
                    return carry

                if few:
                    for z in range(first, sizes[2]):
                        one(z, 0)
                else:
                    lax.fori_loop(first, sizes[2], one, 0)

    each(lambda slot, device: pl.semaphore_signal(barrier, inc=1, device_id=device, device_id_type=MESH))
    prepare(pos_ref, vel_ref, mass_ref, far_ref, cell_ref, ghost_ref, rows_ref, sent_ref, moment_ref)
    own = pltpu.make_async_copy(moment_ref.at[0], every_ref.at[0], own_sem)
    own.start()
    pl.semaphore_wait(barrier, count - 1)

    def around(number):
        offset = (number // 9 - 1, number // 3 % 3 - 1, number % 3 - 1)
        there = tuple(a + b for a, b in zip(here, offset))
        inside = functools.reduce(
            jnp.logical_and, [(a >= 0) & (a < size) for a, size in zip(there, sizes)]
        )
        return there, inside

    def copy(number, there):
        return pltpu.make_async_remote_copy(
            src_ref=sent_ref,
            dst_ref=near_ref.at[26 - number],
            send_sem=send_sems.at[number],
            recv_sem=recv_sems.at[26 - number],
            device_id=there,
            device_id_type=MESH,
        )

    for number in range(27):
        if number != 13:
            there, inside = around(number)

            @pl.when(inside)
            def _():
                copy(number, there).start()

    def share(slot, device):
        pltpu.make_async_remote_copy(
            src_ref=moment_ref.at[0],
            dst_ref=every_ref.at[slot],
            send_sem=moment_sems.at[0],
            recv_sem=moment_sems.at[1],
            device_id=device,
            device_id_type=MESH,
        ).start()

    each(share)
    own.wait()
    rest = every_ref.at[pl.ds(1, count - 1)]
    pltpu.make_async_copy(rest, rest, moment_sems.at[0]).wait()
    pltpu.make_async_copy(rest, rest, moment_sems.at[1]).wait()
    for number in range(27):
        if number != 13:
            there, inside = around(number)

            @pl.when(inside)
            def _():
                pltpu.make_async_copy(sent_ref, sent_ref, send_sems.at[number]).wait()
                pltpu.make_async_copy(near_ref.at[number], near_ref.at[number], recv_sems.at[number]).wait()


def forces(position, velocity, mass):
    norm = jnp.sum(position * position, axis=0, keepdims=True) + 0.5 * SOFTENING
    mixed = jnp.sum(position * velocity, axis=0, keepdims=True)
    nought = jnp.zeros((2, LANES), F32)
    row = lax.broadcasted_iota(jnp.int32, (8, LANES), 0)
    state_row, norm_row, mixed_row = row < 6, row == 6, row == 7
    norm_one, mixed_one = jnp.where(norm_row, 1.0, 0.0), jnp.where(mixed_row, 1.0, 0.0)
    scale = jnp.where(row < 3, -2.0, 0.0)
    left = jnp.concatenate([position, velocity, norm, mixed], axis=0)
    high, middle, low = three(left)
    high_one, middle_one = jnp.where(state_row, high, 1.0), jnp.where(state_row, middle, 1.0)
    left_all = jnp.concatenate([high, high_one, high_one, middle, middle_one, low], axis=0)
    turn = three(jnp.concatenate([-velocity, -position, nought], axis=0))

    def right(parts, mine, one):
        first = jnp.where(mine, one, parts[0])
        second = jnp.where(mine, high, parts[1])
        third = jnp.where(mine, middle, parts[2])
        fourth = jnp.where(mine, low, parts[1])
        return jnp.concatenate([first, second, third, first, fourth, first], axis=0)

    right_all = jnp.concatenate(
        [right((high * scale, middle * scale, low * scale), norm_row, norm_one), right(turn, mixed_row, mixed_one)],
        axis=1,
    )
    pairs = lax.dot_general(
        left_all.astype(BF16),
        right_all.astype(BF16),
        (((0,), (0,)), ((), ())),
        preferred_element_type=F32,
    )
    square, rate = pairs[:, 0:LANES], pairs[:, LANES:]
    inverse = lax.rsqrt(square)
    radius = square * inverse
    inverse2 = inverse * inverse
    near = jnp.clip(OUTER_RADIUS / SPAN - radius * (1.0 / SPAN), 0.0, 1.0)
    weight = (near * near) * (3.0 - 2.0 * near) * (inverse * inverse2)
    turned = weight * (rate * inverse2)
    weight_h = weight.astype(BF16)
    weight_l = (weight - weight_h.astype(F32)).astype(BF16)
    turned_h = turned.astype(BF16)
    turned_l = (turned - turned_h.astype(F32)).astype(BF16)
    matrix = jnp.concatenate(
        [
            jnp.concatenate([weight_h, turned_h], axis=1),
            jnp.concatenate([weight_l, turned_l], axis=1),
        ],
        axis=0,
    )
    values = jnp.where(state_row, left, norm_one) * mass
    values = jnp.concatenate([*three(values), jnp.zeros_like(values)], axis=0).astype(BF16)
    sums = jnp.dot(jnp.concatenate([values, values], axis=1), matrix, preferred_element_type=F32)
    sums = sums[0:8] + sums[8:16] + sums[16:24]
    plain, bent = sums[:, 0:LANES], sums[:, LANES:]
    acceleration = plain[0:3] - position * plain[6:7]
    jerk = plain[3:6] - velocity * plain[6:7] - 3.0 * (bent[0:3] - position * bent[6:7])
    return acceleration, jerk


def far_field(pos_ref, every_ref, far_ref):
    stars = pos_ref.shape[1]
    domains = every_ref.shape[0]
    group = min(32, domains)

    def chunk(number, carry):
        columns = pl.ds(pl.multiple_of(number * LANES, LANES), LANES)
        star = [jnp.broadcast_to(pos_ref[axis : axis + 1, columns], (CELLS, LANES)) for axis in range(3)]

        def some(step, total):
            rows = every_ref[pl.ds(pl.multiple_of(step * group, group), group), :]
            table = rows.T
            for k in range(group):
                mass, *centre = [
                    jnp.broadcast_to(table[c * CELLS : (c + 1) * CELLS, k : k + 1], (CELLS, LANES))
                    for c in range(4)
                ]
                offset = [c - s for c, s in zip(centre, star)]
                square = offset[0] * offset[0] + offset[1] * offset[1] + offset[2] * offset[2] + SOFTENING
                inverse = lax.rsqrt(square)
                fraction = jnp.clip(square * inverse * (1.0 / SPAN) - INNER_RADIUS / SPAN, 0.0, 1.0)
                weight = mass * (fraction * fraction * (3.0 - 2.0 * fraction)) * (inverse * inverse * inverse)
                total = tuple(t + weight * o for t, o in zip(total, offset))
            return total

        total = lax.fori_loop(
            0, domains // group, some, tuple(jnp.zeros((CELLS, LANES), F32) for _ in range(3))
        )
        far_ref[:, columns] = jnp.concatenate([jnp.sum(t, axis=0, keepdims=True) for t in total], axis=0)
        return carry

    lax.fori_loop(0, stars // LANES, chunk, 0)


TOGETHER = 8


def step_stars(
    sizes, capacity, steps_ref, owner_ref, rows_ref, near_ref, index_ref, out_ref, member_ref, slot_ref, order_ref,
):
    blocks, length = index_ref.shape
    out_ref[...] = jnp.zeros_like(out_ref)

    counts = [steps_ref[b] for b in range(blocks)]
    owners = [owner_ref[b] for b in range(blocks)]
    places = [jnp.int32(0)] * blocks
    for b in range(blocks):
        rank = jnp.int32(0)
        for earlier in range(b):
            before = (counts[earlier] <= counts[b]).astype(jnp.int32)
            places[b] = places[b] + before
            places[earlier] = places[earlier] + (1 - before)
            rank = rank + (owners[earlier] == owners[b]).astype(jnp.int32)
        slot_ref[b] = owners[b] * capacity + rank
    for b in range(blocks):
        order_ref[places[b]] = b

    own_chunks = rows_ref.shape[0]
    per = near_ref.shape[1]
    indices = [jnp.broadcast_to(index_ref[b : b + 1, :], (8, LANES)) for b in range(blocks)]
    lane = [i & (LANES - 1) for i in indices]
    chunk = [i >> 7 for i in indices]

    def found(piece, number, carry):
        return tuple(
            jnp.where(c == number, jnp.take_along_axis(piece, l, axis=1), old)
            for c, l, old in zip(chunk, lane, carry)
        )

    carry = tuple(jnp.zeros((8, LANES), F32) for _ in range(blocks))
    for number in range(own_chunks):
        carry = found(rows_ref[number], number, carry)
    def reach(slot, carry):
        for part in range(per):
            carry = found(near_ref[slot, part], own_chunks + slot * per + part, carry)
        return carry

    bounds = []
    for axis, size in zip(AXES, sizes):
        at = lax.axis_index(axis)
        bounds.append((jnp.where(at > 0, 0, 1), jnp.where(at < size - 1, 3, 2)))
    (low_x, high_x), (low_y, high_y), (low_z, high_z) = bounds
    wide_y, wide_z = high_y - low_y, high_z - low_z

    def visit(step, carry):
        number = (low_x + step // (wide_y * wide_z)) * 9
        number = number + (low_y + step // wide_z % wide_y) * 3 + low_z + step % wide_z
        return reach(number, carry)

    carry = lax.fori_loop(0, (high_x - low_x) * wide_y * wide_z, visit, carry)
    for b, value in enumerate(carry):
        member_ref[b] = value

    def bunch(number, carry):
        names = [order_ref[number * TOGETHER + g] for g in range(TOGETHER)]
        counts = [steps_ref[name] for name in names]
        most = counts[-1]
        data = []
        state = []
        for name, n in zip(names, counts):
            value = member_ref[name]
            middle = jnp.sum(value[0:6], axis=1, keepdims=True) * (1.0 / length)
            moved = value[0:6] - middle
            mass = value[6:7]
            steps = jnp.full((3, LANES), n, jnp.int32)
            width = TIME_STEP / jnp.maximum(steps.astype(F32), 1.0)
            drift = jnp.broadcast_to(middle[3:6], (3, LANES)) * TIME_STEP
            data.append((mass, steps, width, drift, moved))
            position, velocity = moved[0:3], moved[3:6]
            state.append((position, velocity, *forces(position, velocity, mass)))

        def advance(step, state):
            after = []
            for (mass, steps, width, drift, moved), (position, velocity, acc, jerk) in zip(data, state):
                squared = width * width
                predicted = (
                    position + width * velocity + 0.5 * squared * acc + squared * width * (1.0 / 6.0) * jerk
                )
                predicted_vel = velocity + width * acc + 0.5 * squared * jerk
                acc_new, jerk_new = forces(predicted, predicted_vel, mass)
                velocity_new = (
                    velocity + 0.5 * width * (acc + acc_new) + squared * (1.0 / 12.0) * (jerk - jerk_new)
                )
                position_new = (
                    position + 0.5 * width * (velocity + velocity_new) + squared * (1.0 / 12.0) * (acc - acc_new)
                )
                live = steps > step
                after.append(
                    tuple(
                        jnp.where(live, new, old)
                        for new, old in (
                            (position_new, position), (velocity_new, velocity), (acc_new, acc), (jerk_new, jerk),
                        )
                    )
                )
            return tuple(after)

        state = lax.fori_loop(0, most, advance, tuple(state))
        for name, (mass, steps, width, drift, moved), (position, velocity, acc, jerk) in zip(names, data, state):
            change = jnp.concatenate([position - moved[0:3] + drift, velocity - moved[3:6]], axis=0)
            at = pl.multiple_of(slot_ref[name] * length, length)
            out_ref[:, pl.ds(at, length)] = change
        return carry

    lax.fori_loop(0, blocks // TOGETHER, bunch, 0)


def deliver(lanes, packed_ref, pos_ref, every_ref, out_ref, far_ref, own_sem, sems):
    here = tuple(lax.axis_index(axis) for axis in AXES)
    me = here[2]
    part = packed_ref.shape[1] // lanes
    barrier = pltpu.get_barrier_semaphore()

    def columns(number):
        return pl.ds(pl.multiple_of(number * part, LANES), part)

    own = pltpu.make_async_copy(packed_ref.at[:, columns(me)], out_ref.at[:, columns(me)], own_sem)
    own.start()

    def other(step):
        there = lax.rem(me + step, lanes)
        return there, (here[0], here[1], there)

    def greet(step, carry):
        pl.semaphore_signal(barrier, inc=1, device_id=other(step)[1], device_id_type=MESH)
        return carry

    lax.fori_loop(1, lanes, greet, 0)
    pl.semaphore_wait(barrier, lanes - 1)

    def send(step, carry):
        there, device = other(step)
        pltpu.make_async_remote_copy(
            src_ref=packed_ref.at[:, columns(there)],
            dst_ref=out_ref.at[:, columns(me)],
            send_sem=sems.at[0],
            recv_sem=sems.at[1],
            device_id=device,
            device_id_type=MESH,
        ).start()
        return carry

    lax.fori_loop(1, lanes, send, 0)
    far_field(pos_ref, every_ref, far_ref)
    own.wait()
    rest = packed_ref.at[:, pl.ds(0, (lanes - 1) * part)]
    pltpu.make_async_copy(rest, rest, sems.at[0]).wait()
    pltpu.make_async_copy(rest, rest, sems.at[1]).wait()


def finish(far_ref, arrived_ref, far_out_ref, out_ref, sems):
    first = pltpu.make_async_copy(arrived_ref, out_ref, sems.at[0])
    second = pltpu.make_async_copy(far_ref, far_out_ref, sems.at[1])
    first.start()
    second.start()
    first.wait()
    second.wait()


def vmem(count):
    return [pl.BlockSpec(memory_space=pltpu.VMEM)] * count


def on_device(
    sizes, positions, velocities, star_mass, far_previous, cell_index, ghost_list, block_index, block_owner, substeps
):
    lanes = sizes[2]
    domains = sizes[0] * sizes[1] * sizes[2]
    blocks, length = block_index.shape
    capacity = max(2, 2 * BLOCKS_DEV // lanes)
    stars, ghosts = positions.shape[1], ghost_list.shape[0]
    shape = jax.ShapeDtypeStruct
    sent = (ghosts // LANES, 8, LANES)
    rows, near, every = pl.pallas_call(
        functools.partial(exchange, sizes),
        out_shape=(
            shape((stars // LANES, 8, LANES), F32),
            shape((27, *sent), F32),
            shape((domains, 1, LANES), F32),
        ),
        in_specs=vmem(6),
        out_specs=tuple(vmem(3)),
        scratch_shapes=[
            pltpu.VMEM(sent, F32),
            pltpu.VMEM((1, 1, LANES), F32),
            pltpu.SemaphoreType.DMA,
            pltpu.SemaphoreType.DMA((2,)),
            pltpu.SemaphoreType.DMA((27,)),
            pltpu.SemaphoreType.DMA((27,)),
        ],
        compiler_params=pltpu.CompilerParams(collective_id=0, has_side_effects=True),
        name="exchange",
    )(
        positions,
        velocities,
        star_mass.reshape(1, stars),
        far_previous,
        cell_index.reshape(1, stars),
        ghost_list.reshape(1, ghosts),
    )
    smem = pl.BlockSpec(memory_space=pltpu.SMEM)
    packed = pl.pallas_call(
        functools.partial(step_stars, sizes, capacity),
        out_shape=shape((6, lanes * capacity * length), F32),
        in_specs=[smem, smem, *vmem(3)],
        out_specs=vmem(1)[0],
        scratch_shapes=[
            pltpu.VMEM((blocks, 8, LANES), F32),
            pltpu.SMEM((blocks,), jnp.int32),
            pltpu.SMEM((blocks,), jnp.int32),
        ],
        name="step_stars",
    )(substeps, block_owner.reshape(blocks), rows, near, block_index)
    arrived, far_acc = pl.pallas_call(
        functools.partial(deliver, lanes),
        out_shape=(shape(packed.shape, F32), shape((3, stars), F32)),
        in_specs=vmem(3),
        out_specs=tuple(vmem(2)),
        scratch_shapes=[pltpu.SemaphoreType.DMA, pltpu.SemaphoreType.DMA((2,))],
        compiler_params=pltpu.CompilerParams(collective_id=1, has_side_effects=True),
        name="deliver",
    )(packed, positions, every.reshape(domains, LANES))
    return pl.pallas_call(
        finish,
        out_shape=(shape(far_acc.shape, F32), shape(arrived.shape, F32)),
        in_specs=vmem(2),
        out_specs=(pl.BlockSpec(memory_space=pl.ANY), pl.BlockSpec(memory_space=pl.ANY)),
        scratch_shapes=[pltpu.SemaphoreType.DMA((2,))],
        name="finish",
    )(far_acc, arrived)


def solution(mesh):
    split = P(AXES)
    wide = P(None, AXES)
    tall = P(AXES, None)
    return jax.shard_map(
        functools.partial(on_device, tuple(mesh.shape[axis] for axis in AXES)),
        mesh=mesh,
        in_specs=(wide, wide, split, wide, split, split, tall, tall, split),
        out_specs=(wide, wide),
        check_vma=False,
    )
```

profile of v0, /device:TPU:0, one launch (start us, length us, event | category | flops | bytes accessed | tf_op | source)
XLA Modules:
  0.0 36.0 jit_solution(17258958649992584624)
XLA Ops:
  0.6 11.8 %exchange.1 = (f32[4,8,128]{2,1,0:T(8,128)}, f32[27,2,8,128]{3,2,1,0:T(8,128)}, f32[32,1,128]{2,1,0:T(1,128)}) custom-call(f32[3,512]{1,0:T(4,128)} %pos_ref.3, f32[3,512]{1,0:T(4,128)} %vel_ref.1, f32[1,512]{1,0:T(1,128)} %bitcast.6, f32[3,512]{1,0:T(4,128)} %far_ref.1, s32[1,512]{1,0:T(1,128)} %bitcast.7, s32[1,256]{1,0:T(1,128)} %bitcast.8), custom_call_target="tpu_custom_call" | custom-call | tf_op jit(solution)/shard_map/exchange/pallas_call | solution.py:426
  12.4 16.1 %step_stars.1.packed_ref = f32[6,4096]{1,0:T(8,128)} custom-call(s32[16]{0:T(128)} %steps_ref.1, s32[16]{0:T(128)} %bitcast.9, f32[4,8,128]{2,1,0:T(8,128)} %get-tuple-element.7.rows_ref, f32[27,2,8,128]{3,2,1,0:T(8,128)} %get-tuple-element.8.near_ref, s32[16,128]{1,0:T(8,128)} %index_ref.1), custom_call_target="tpu_custom_call" | custom-call | tf_op jit(solution)/shard_map/step_stars/pallas_call | solution.py:454
  28.5 5.9 %deliver.1 = (f32[6,4096]{1,0:T(8,128)}, f32[3,512]{1,0:T(4,128)}) custom-call(f32[6,4096]{1,0:T(8,128)} %step_stars.1.packed_ref, f32[3,512]{1,0:T(4,128)} %pos_ref.3, f32[32,128]{1,0:T(8,128)} %bitcast.5), custom_call_target="tpu_custom_call" | custom-call | tf_op jit(solution)/shard_map/deliver/pallas_call | solution.py:466
  34.4 1.6 %finish.1 = (f32[3,512]{1,0:T(4,128)}, f32[6,4096]{1,0:T(8,128)}) custom-call(f32[3,512]{1,0:T(4,128)} %get-tuple-element.10.far_ref, f32[6,4096]{1,0:T(8,128)} %get-tuple-element.11.arrived_ref), custom_call_target="tpu_custom_call" | custom-call | tf_op jit(solution)/shard_map/finish/pallas_call | solution.py:475
where the time goes:
time: 35.8 us; the launch traced here: 36 us
  Pallas kernels  35.4 us (99%)
  between operations  0.65 us (2%)
    pallas_call x1, Pallas kernels, on_device(): pl.pallas_call(functools.partial(step_stars, sizes, capacity), out_shape=...  16.1 us
    pallas_call x1, Pallas kernels, on_device(): pl.pallas_call(functools.partial(exchange, sizes), out_shape=(shape((star...  11.8 us
    pallas_call x1, Pallas kernels, on_device(): pl.pallas_call(functools.partial(deliver, lanes), out_shape=(shape(packed...  5.92 us
    pallas_call x1, Pallas kernels, on_device(): pl.pallas_call(finish, out_shape=(shape(far_acc.shape, F32), shape(arrive...  1.6 us

commit v1 on v0

v1 whole, which is shorter than its diff:
```python
import functools

import jax
import jax.numpy as jnp
from jax import lax
from jax.experimental import pallas as pl
from jax.experimental.pallas import tpu as pltpu
from jax.sharding import PartitionSpec as P

CELLS = 16
BLOCKS_DEV = 16
SUBMAX = 8
TOGETHER = 8
AXES = ("gx", "gy", "gz")
MESH = pl.DeviceIdType.MESH
LANES = 128

SOFTENING = 0.0025
INNER_RADIUS = 0.25
OUTER_RADIUS = 1.0
TIME_STEP = 0.25
SPAN = OUTER_RADIUS - INNER_RADIUS
CUBIC = 2.0 / SPAN**3

BF16 = jnp.bfloat16
F32 = jnp.float32
I32 = jnp.int32


def iota(shape, axis):
    return lax.broadcasted_iota(I32, shape, axis)


def halves(value):
    high = value.astype(BF16).astype(F32)
    return high, value - high


def three(value):
    high, rest = halves(value)
    middle, low = halves(rest)
    return high, middle, low


def own_rows(position, kicked, mass):
    return jnp.concatenate([position, mass, kicked, jnp.zeros_like(mass)], axis=0)


def moments(position, mass, cell):
    stars = mass.shape[1]
    number = iota((LANES, stars), 0)
    member = jnp.where(jnp.broadcast_to(cell, (LANES, stars)) == number, 1.0, 0.0).astype(BF16)
    weighted = jnp.concatenate([mass, position * mass, jnp.zeros((4, stars), F32)], axis=0)
    parts = jnp.concatenate([*three(weighted), jnp.zeros_like(weighted)], axis=0).astype(BF16)
    sums = lax.dot_general(parts, member, (((1,), (1,)), ((), ())), preferred_element_type=F32)
    sums = sums[0:8] + sums[8:16] + sums[16:24]
    inside = iota((1, LANES), 1) < CELLS
    total = jnp.where(inside, sums[0:1], 0.0)
    packed = total
    for axis in range(3):
        centre = jnp.where(inside, sums[axis + 1 : axis + 2] / jnp.where(inside, total, 1.0), 0.0)
        packed = packed + pltpu.roll(centre, (axis + 1) * CELLS, 1)
    return packed


def far_left(cells):
    high, low = halves(cells)
    fourth = iota(cells.shape, 0) == 3
    ones = [jnp.where(fourth, 1.0, part) for part in (high, low)]
    return jnp.concatenate([high, low, *ones], axis=0).astype(BF16)


def far_right(stars):
    high, low = halves(stars)
    fourth = iota(stars.shape, 0) == 3
    scaled = [jnp.where(fourth, 1.0, high * -2.0), jnp.where(fourth, 1.0, high * -2.0)]
    scaled += [jnp.where(fourth, part, low * -2.0) for part in (low, high)]
    return jnp.concatenate(scaled, axis=0).astype(BF16)


def with_norm(point, extra):
    norm = jnp.sum(point * point, axis=0, keepdims=True) + extra
    return jnp.concatenate([point, norm], axis=0)


def arrange(capacity, counts, owners, index):
    blocks, length = index.shape
    shape = (blocks, blocks)
    row, column = iota(shape, 0), iota(shape, 1)

    def across(value):
        along = jnp.broadcast_to(value.astype(F32), shape)
        return along, jnp.sum(jnp.where(row == column, along, 0.0), axis=1, keepdims=True)

    count_row, count_col = across(counts)
    owner_row, owner_col = across(owners)
    before = (count_col > count_row) | ((count_col == count_row) & (row < column))
    place = jnp.sum(jnp.where(before, 1.0, 0.0), axis=0, keepdims=True)
    turn = jnp.where(place == row.astype(F32), 1.0, 0.0).astype(BF16)
    rank = jnp.sum(jnp.where((owner_row == owner_col) & (column < row), 1.0, 0.0), axis=1, keepdims=True)
    slot = owner_col * capacity + rank
    at = iota((blocks, LANES), 1)
    facts = jnp.where(at == 0, count_col, jnp.where(at == 1, slot, 0.0))
    table = jnp.concatenate([(index & (LANES - 1)).astype(F32), (index >> 7).astype(F32), facts], axis=1)
    table = jnp.dot(turn, table.astype(BF16), preferred_element_type=F32)
    lane, chunk = table[:, 0:length].astype(I32), table[:, length : 2 * length].astype(I32)
    facts = table[:, 2 * length :]
    going = jnp.sum(jnp.where(facts[:, 0:1] > at.astype(F32), 1.0, 0.0), axis=0, keepdims=True)
    going = jnp.where(going > 0.0, jnp.maximum(going, float(TOGETHER)), 0.0)
    items = jnp.sum(going, axis=1, keepdims=True)
    going = jnp.where(iota((1, LANES), 1) == LANES - 1, items, going)
    plan = jnp.concatenate([facts, jnp.broadcast_to(going, (8, LANES))], axis=0).astype(I32)
    return lane, chunk, plan


def exchange(
    sizes, capacity,
    pos_hbm, vel_hbm, mass_hbm, far_hbm, cell_hbm, ghost_hbm, index_hbm, owner_hbm, steps_hbm,
    member_ref, plan_ref, star_ref, right_ref, every_ref,
    pos_ref, vel_ref, mass_ref, prev_ref, cell_ref, ghost_ref, index_ref, owner_ref, count_ref,
    near_ref, sent_ref, where_ref, in_sems, moment_sems, send_sems, recv_sems,
):
    domains = sizes[0] * sizes[1] * sizes[2]
    blocks = index_ref.shape[0]
    here = tuple(lax.axis_index(axis) for axis in AXES)
    loads = [
        pltpu.make_async_copy(source, into, in_sems.at[number])
        for number, (source, into) in enumerate(
            (
                (pos_hbm, pos_ref), (vel_hbm, vel_ref), (mass_hbm, mass_ref), (far_hbm, prev_ref), (cell_hbm, cell_ref),
                (ghost_hbm, ghost_ref), (index_hbm, index_ref), (owner_hbm, owner_ref), (steps_hbm, count_ref),
            )
        )
    ]
    for load in loads:
        load.start()
    barrier = pltpu.get_barrier_semaphore()

    turned = [[lax.rem(at + k, size) for k in range(size)] for at, size in zip(here[:2], sizes)]
    few = sizes[2] <= 4

    def each(act):
        for x, at_x in enumerate(turned[0]):
            for y, at_y in enumerate(turned[1]):
                first = 1 if x == 0 and y == 0 else 0

                def one(z, carry):
                    act((x * sizes[1] + y) * sizes[2] + z, (at_x, at_y, lax.rem(here[2] + z, sizes[2])))
                    return carry

                if few:
                    for z in range(first, sizes[2]):
                        one(z, 0)
                else:
                    lax.fori_loop(first, sizes[2], one, 0)

    each(lambda slot, device: pl.semaphore_signal(barrier, inc=1, device_id=device, device_id_type=MESH))
    for load in loads:
        load.wait()

    stars = pos_ref.shape[1]
    position, mass = pos_ref[...], mass_ref[...]
    kicked = vel_ref[...] + prev_ref[...] * (0.5 * TIME_STEP)
    rows = own_rows(position, kicked, mass)
    own = [rows[:, n * LANES : (n + 1) * LANES] for n in range(stars // LANES)]
    per = ghost_ref.shape[1] // LANES
    for number in range(per):
        index = jnp.broadcast_to(ghost_ref[:, number * LANES : (number + 1) * LANES], (8, LANES))
        at, part = index & (LANES - 1), index >> 7
        found = jnp.zeros((8, LANES), F32)
        for n, piece in enumerate(own):
            found = jnp.where(part == n, jnp.take_along_axis(piece, at, axis=1), found)
        sent_ref[number] = found
    every_ref[0] = moments(position, mass, cell_ref[...])

    middle = [at.astype(F32) + 0.5 for at in here]
    shift = jnp.where(
        iota((3, stars), 0) == 0, middle[0], jnp.where(iota((3, stars), 0) == 1, middle[1], middle[2])
    )
    star = with_norm(position - shift, 0.0)
    star_ref[...] = star
    right_ref[...] = far_right(star)

    lane, chunk, plan = arrange(capacity, count_ref[...], owner_ref[...], index_ref[...])
    plan_ref[...] = plan
    where_ref[0] = lane
    where_ref[1] = chunk

    def gather(pieces, first):
        for start in range(0, blocks, 8):
            names = range(start, min(start + 8, blocks))
            lanes = [jnp.broadcast_to(where_ref[0, b : b + 1, :], (8, LANES)) for b in names]
            chunks = [jnp.broadcast_to(where_ref[1, b : b + 1, :], (8, LANES)) for b in names]
            held = [jnp.zeros((8, LANES), F32) if first else member_ref[b] for b in names]
            for number, read in pieces:
                piece = read()
                held = [
                    jnp.where(c == number, jnp.take_along_axis(piece, l, axis=1), old)
                    for c, l, old in zip(chunks, lanes, held)
                ]
            for b, value in zip(names, held):
                member_ref[b] = value

    gather([(n, lambda piece=piece: piece) for n, piece in enumerate(own)], True)
    pl.semaphore_wait(barrier, domains - 1)

    def around(number):
        offset = (number // 9 - 1, number // 3 % 3 - 1, number % 3 - 1)
        there = tuple(a + b for a, b in zip(here, offset))
        inside = functools.reduce(jnp.logical_and, [(a >= 0) & (a < size) for a, size in zip(there, sizes)])
        return there, inside

    for number in range(27):
        if number != 13:
            there, inside = around(number)

            @pl.when(inside)
            def _():
                pltpu.make_async_remote_copy(
                    src_ref=sent_ref,
                    dst_ref=near_ref.at[26 - number],
                    send_sem=send_sems.at[number],
                    recv_sem=recv_sems.at[26 - number],
                    device_id=there,
                    device_id_type=MESH,
                ).start()

    def share(slot, device):
        pltpu.make_async_remote_copy(
            src_ref=every_ref.at[0],
            dst_ref=every_ref.at[slot],
            send_sem=moment_sems.at[0],
            recv_sem=moment_sems.at[1],
            device_id=device,
            device_id_type=MESH,
        ).start()

    each(share)

    def settle(number):
        there, inside = around(number)

        @pl.when(inside)
        def _():
            pltpu.make_async_copy(near_ref.at[number], near_ref.at[number], recv_sems.at[number]).wait()

    def reads(slot):
        return [
            (len(own) + slot * per + part, lambda part=part: near_ref[slot, part]) for part in range(per)
        ]

    low = jnp.where(here[2] > 0, 0, 1)
    for x in (1, 0, 2):
        for number in range(x * 9, x * 9 + 9):
            if number != 13:
                settle(number)
        pieces = []
        for y in range(3):
            at = x * 9 + y * 3
            if sizes[2] != 2:
                slots = [at + z for z in range(3) if at + z != 13]
            elif at == 12:
                slots = [at + 2 * low]
            else:
                slots = [at + low, at + low + 1]
            for slot in slots:
                pieces += reads(slot)
        gather(pieces, False)

    rest = every_ref.at[pl.ds(1, domains - 1)]
    pltpu.make_async_copy(rest, rest, moment_sems.at[0]).wait()
    pltpu.make_async_copy(rest, rest, moment_sems.at[1]).wait()
    for number in range(27):
        if number != 13:
            there, inside = around(number)

            @pl.when(inside)
            def _():
                pltpu.make_async_copy(sent_ref, sent_ref, send_sems.at[number]).wait()


class Rows:
    def __init__(self):
        row = iota((8, LANES), 0)
        self.upper = row < 4
        self.third = row == 3
        self.seventh = row == 7
        self.spare = self.third | self.seventh
        self.used = jnp.where(self.spare, 0.0, 1.0)
        self.first_used = jnp.where(row < 3, 1.0, 0.0)
        self.last_used = jnp.where(self.upper | self.spare, 0.0, 1.0)
        self.soften = jnp.where(self.third, 0.5 * SOFTENING, 0.0)
        self.double = self.first_used * -2.0
        self.turn = -self.used
        self.thrice = self.last_used * 3.0


def forces(rows, state, mass):
    swapped = pltpu.roll(state, 4, 0)
    product = state * jnp.where(rows.upper, state, swapped)
    norms = pltpu.roll(product, 1, 0) + pltpu.roll(product, 2, 0) + pltpu.roll(product, 3, 0) + rows.soften
    high, low = halves(jnp.where(rows.spare, norms, state))
    left = [high, low, jnp.where(rows.spare, 1.0, high), jnp.where(rows.spare, 1.0, low)]

    def right(one, high_part, low_part):
        lead = jnp.where(one, 1.0, high_part)
        return [lead, lead, jnp.where(one, low, low_part), jnp.where(one, high, low_part)]

    square_side = right(rows.third, high * rows.double, low * rows.double)
    rate_side = right(rows.seventh, pltpu.roll(high, 4, 0) * rows.turn, pltpu.roll(low, 4, 0) * rows.turn)
    pairs = lax.dot_general(
        jnp.concatenate(left, axis=0).astype(BF16),
        jnp.concatenate(
            [jnp.concatenate(square_side, axis=0).astype(BF16), jnp.concatenate(rate_side, axis=0).astype(BF16)], axis=1
        ),
        (((0,), (0,)), ((), ())),
        preferred_element_type=F32,
    )
    square, rate = pairs[:, 0:LANES], pairs[:, LANES:]
    inverse = lax.rsqrt(square)
    inverse2 = inverse * inverse
    near = jnp.clip(OUTER_RADIUS - square * inverse, 0.0, SPAN)
    weight = (near * near) * (1.5 * SPAN - near) * (inverse * inverse2)
    turned = weight * (rate * inverse2)
    matrix = []
    for value in (weight, turned):
        high_part = value.astype(BF16)
        matrix.append(jnp.concatenate([high_part, (value - high_part.astype(F32)).astype(BF16)], axis=0))
    matrix = jnp.concatenate(matrix, axis=1)
    values = jnp.concatenate(halves(jnp.where(rows.third, 1.0, state) * mass), axis=0).astype(BF16)
    sums = jnp.dot(jnp.concatenate([values, values], axis=1), matrix, preferred_element_type=F32)
    sums = sums[0:8] + sums[8:16]
    plain, bent = sums[:, 0:LANES], sums[:, LANES:]
    straight = plain - state * jnp.broadcast_to(plain[3:4], (8, LANES))
    curved = bent - state * jnp.broadcast_to(bent[3:4], (8, LANES))
    return straight - rows.thrice * pltpu.roll(curved, 4, 0)


def step_stars(
    plan_vmem, member_ref, out_ref, plan_ref, state_ref, force_ref, mass_ref, origin_ref, sem,
):
    blocks = member_ref.shape[0]
    fetch = pltpu.make_async_copy(plan_vmem, plan_ref, sem)
    fetch.start()
    out_ref[...] = jnp.zeros_like(out_ref)
    rows = Rows()

    def begin(number, carry):
        for g in range(TOGETHER):
            name = number * TOGETHER + g
            value = member_ref[name]
            middle = jnp.sum(value, axis=1, keepdims=True) * (1.0 / LANES)
            middle = jnp.broadcast_to(middle, (8, LANES))
            state = (value - middle) * rows.used
            mass = jnp.broadcast_to(value[3:4], (8, LANES)) * CUBIC
            state_ref[name] = state
            mass_ref[name] = mass
            origin_ref[name] = state - rows.first_used * pltpu.roll(middle, 4, 0) * TIME_STEP
            force_ref[name] = forces(rows, state, mass)
        return carry

    lax.fori_loop(0, blocks // TOGETHER, begin, 0)
    fetch.wait()

    def advance(number, carry):
        step, place = carry
        limit = plan_ref[blocks, step]
        names, widths = [], []
        for g in range(TOGETHER):
            over = place + g >= limit
            name = jnp.where(over, place + g - limit, place + g)
            count = plan_ref[name, 0]
            live = count > step + over.astype(I32)
            names.append(name)
            widths.append(jnp.where(live, TIME_STEP / count.astype(F32), 0.0))
        fresh = []
        for name, width in zip(names, widths):
            state, force, mass = state_ref[name], force_ref[name], mass_ref[name]
            h = rows.used * width
            squared = h * h
            moving = h * jnp.where(rows.upper, pltpu.roll(state, 4, 0), pltpu.roll(force, 4, 0))
            cubed = squared * h * (rows.first_used * (1.0 / 6.0))
            predicted = state + moving + (0.5 * squared) * force + cubed * pltpu.roll(force, 4, 0)
            force_new = forces(rows, predicted, mass)
            gap = force - force_new
            half = 0.5 * h
            change = moving + squared * (1.0 / 12.0) * gap - half * rows.last_used * pltpu.roll(gap, 4, 0)
            change = change + half * rows.first_used * pltpu.roll(change, 4, 0)
            fresh.append((name, state + change, force_new))
        for name, state, force in fresh:
            state_ref[name] = state
            force_ref[name] = force
        place = place + TOGETHER
        over = place >= limit
        return jnp.where(over, step + 1, step), jnp.where(over, place - limit, place)

    items = plan_ref[blocks, LANES - 1]
    lax.fori_loop(0, (items + (TOGETHER - 1)) // TOGETHER, advance, (jnp.int32(0), jnp.int32(0)))
    for name in range(blocks):
        change = state_ref[name] - origin_ref[name]
        at = pl.multiple_of(plan_ref[name, 1] * LANES, LANES)
        out_ref[:, pl.ds(at, LANES)] = jnp.concatenate([change[0:3], change[4:7]], axis=0)


def far_field(here, star_ref, right_ref, every_ref, far_ref):
    stars = star_ref.shape[1]
    domains = every_ref.shape[0]
    row, column = iota((8, LANES), 0), iota((8, LANES), 1)
    middle = [at.astype(F32) + 0.5 for at in here]
    shift = jnp.where(row == 6, middle[0], jnp.where(row == 5, middle[1], jnp.where(row == 4, middle[2], 0.0)))

    def some(number, total):
        table = every_ref[pl.ds(pl.multiple_of(number * 8, 8), 8), :]
        cells = jnp.zeros((8, LANES), F32)
        for j in range(8):
            spread = jnp.broadcast_to(table[j : j + 1], (8, LANES))
            spread = pltpu.roll(pltpu.roll(spread, CELLS * ((j + 1) % 8), 1), 0, 1, stride=CELLS, stride_axis=0)
            cells = jnp.where(column // CELLS == j, spread, cells)
        cells = cells - shift
        mass = cells[7:8] * CUBIC
        centre = jnp.concatenate([cells[6:7], cells[5:6], cells[4:5]], axis=0)
        left = far_left(with_norm(centre, SOFTENING))
        square = lax.dot_general(left, right_ref[...], (((0,), (0,)), ((), ())), preferred_element_type=F32)
        inverse = lax.rsqrt(square)
        gone = jnp.clip(square * inverse - INNER_RADIUS, 0.0, SPAN)
        weight = (gone * gone) * (1.5 * SPAN - gone) * (inverse * inverse * inverse)
        high = weight.astype(BF16)
        matrix = jnp.concatenate([high, (weight - high.astype(F32)).astype(BF16)], axis=0)
        values = jnp.concatenate([centre * mass, mass, jnp.zeros((4, LANES), F32)], axis=0)
        values = jnp.concatenate(halves(values), axis=0).astype(BF16)
        sums = jnp.dot(jnp.concatenate([values, values], axis=1), matrix, preferred_element_type=F32)
        return total + sums[0:8] + sums[8:16]

    total = lax.fori_loop(0, domains // 8, some, jnp.zeros((8, stars), F32))
    far_ref[...] = total[0:3] - star_ref[0:3, :] * total[3:4]


def deliver(lanes, packed_ref, star_ref, right_ref, every_ref, out_ref, far_ref, own_sem, sems):
    here = tuple(lax.axis_index(axis) for axis in AXES)
    me = here[2]
    part = packed_ref.shape[1] // lanes
    barrier = pltpu.get_barrier_semaphore()

    def columns(number):
        return pl.ds(pl.multiple_of(number * part, LANES), part)

    def other(step):
        there = lax.rem(me + step, lanes)
        return there, (here[0], here[1], there)

    def greet(step, carry):
        pl.semaphore_signal(barrier, inc=1, device_id=other(step)[1], device_id_type=MESH)
        return carry

    lax.fori_loop(1, lanes, greet, 0)
    own = pltpu.make_async_copy(packed_ref.at[:, columns(me)], out_ref.at[:, columns(me)], own_sem)
    own.start()
    pl.semaphore_wait(barrier, lanes - 1)

    def send(step, carry):
        there, device = other(step)
        pltpu.make_async_remote_copy(
            src_ref=packed_ref.at[:, columns(there)],
            dst_ref=out_ref.at[:, columns(me)],
            send_sem=sems.at[0],
            recv_sem=sems.at[1],
            device_id=device,
            device_id_type=MESH,
        ).start()
        return carry

    lax.fori_loop(1, lanes, send, 0)
    far_field(here, star_ref, right_ref, every_ref, far_ref)
    own.wait()
    rest = packed_ref.at[:, pl.ds(0, (lanes - 1) * part)]
    pltpu.make_async_copy(rest, rest, sems.at[0]).wait()
    pltpu.make_async_copy(rest, rest, sems.at[1]).wait()


def finish(far_ref, arrived_ref, far_out_ref, out_ref, sems):
    first = pltpu.make_async_copy(arrived_ref, out_ref, sems.at[0])
    second = pltpu.make_async_copy(far_ref, far_out_ref, sems.at[1])
    first.start()
    second.start()
    first.wait()
    second.wait()


def vmem(count):
    return [pl.BlockSpec(memory_space=pltpu.VMEM)] * count


def hbm(count):
    return [pl.BlockSpec(memory_space=pltpu.HBM)] * count


def params(**more):
    return pltpu.CompilerParams(vmem_limit_bytes=16 * 1024 * 1024, **more)


def on_device(
    sizes, positions, velocities, star_mass, far_previous, cell_index, ghost_list, block_index, block_owner, substeps
):
    lanes = sizes[2]
    domains = sizes[0] * sizes[1] * sizes[2]
    blocks, length = block_index.shape
    capacity = max(2, 2 * BLOCKS_DEV // lanes)
    stars, ghosts = positions.shape[1], ghost_list.shape[0]
    shape = jax.ShapeDtypeStruct
    sent = (ghosts // LANES, 8, LANES)
    member, plan, star, right, every = pl.pallas_call(
        functools.partial(exchange, sizes, capacity),
        out_shape=(
            shape((blocks, 8, LANES), F32),
            shape((blocks + 8, LANES), I32),
            shape((4, stars), F32),
            shape((16, stars), BF16),
            shape((domains, 1, LANES), F32),
        ),
        in_specs=hbm(9),
        out_specs=tuple(vmem(5)),
        scratch_shapes=[
            pltpu.VMEM((3, stars), F32),
            pltpu.VMEM((3, stars), F32),
            pltpu.VMEM((1, stars), F32),
            pltpu.VMEM((3, stars), F32),
            pltpu.VMEM((1, stars), I32),
            pltpu.VMEM((1, ghosts), I32),
            pltpu.VMEM((blocks, length), I32),
            pltpu.VMEM((1, blocks), I32),
            pltpu.VMEM((1, blocks), I32),
            pltpu.VMEM((27, *sent), F32),
            pltpu.VMEM(sent, F32),
            pltpu.VMEM((2, blocks, length), I32),
            pltpu.SemaphoreType.DMA((9,)),
            pltpu.SemaphoreType.DMA((2,)),
            pltpu.SemaphoreType.DMA((27,)),
            pltpu.SemaphoreType.DMA((27,)),
        ],
        compiler_params=params(collective_id=0, has_side_effects=True),
        name="exchange",
    )(
        *(
            pltpu.with_memory_space_constraint(array, pltpu.HBM)
            for array in (
                positions,
                velocities,
                star_mass.reshape(1, stars),
                far_previous,
                cell_index.reshape(1, stars),
                ghost_list.reshape(1, ghosts),
                block_index,
                block_owner.reshape(1, blocks),
                substeps.reshape(1, blocks),
            )
        )
    )
    block = pltpu.VMEM((blocks, 8, LANES), F32)
    packed = pl.pallas_call(
        step_stars,
        out_shape=shape((6, lanes * capacity * length), F32),
        in_specs=vmem(2),
        out_specs=vmem(1)[0],
        scratch_shapes=[pltpu.SMEM(plan.shape, I32), block, block, block, block, pltpu.SemaphoreType.DMA],
        compiler_params=params(),
        name="step_stars",
    )(plan, member)
    arrived, far_acc = pl.pallas_call(
        functools.partial(deliver, lanes),
        out_shape=(shape(packed.shape, F32), shape((3, stars), F32)),
        in_specs=vmem(4),
        out_specs=tuple(vmem(2)),
        scratch_shapes=[pltpu.SemaphoreType.DMA, pltpu.SemaphoreType.DMA((2,))],
        compiler_params=params(collective_id=1, has_side_effects=True),
        name="deliver",
    )(packed, star, right, every.reshape(domains, LANES))
    return pl.pallas_call(
        finish,
        out_shape=(shape(far_acc.shape, F32), shape(arrived.shape, F32)),
        in_specs=vmem(2),
        out_specs=tuple(hbm(2)),
        scratch_shapes=[pltpu.SemaphoreType.DMA((2,))],
        compiler_params=params(),
        name="finish",
    )(far_acc, arrived)


def solution(mesh):
    split = P(AXES)
    wide = P(None, AXES)
    tall = P(AXES, None)
    return jax.shard_map(
        functools.partial(on_device, tuple(mesh.shape[axis] for axis in AXES)),
        mesh=mesh,
        in_specs=(wide, wide, split, wide, split, split, tall, tall, split),
        out_specs=(wide, wide),
        check_vma=False,
    )
```

time: 35.8 us -> 28.2 us (0.79); the launches traced: 36 us -> 28 us
  Pallas kernels: 35.4 us -> 27.3 us
    pallas_call x2, Pallas kernels: 27.9 us -> 22.3 us  [the longest x1 12.1 us: on_device(): pl.pallas_call(functools.partial(exchange, sizes, capacity), out_shape=(s...]
    pallas_call x1, Pallas kernels: 5.92 us -> 4.33 us  [on_device(): pl.pallas_call(functools.partial(deliver, lanes), out_shape=(shape(packed...]
    pallas_call x1, Pallas kernels: 1.6 us -> 0.68 us  [on_device(): pl.pallas_call(finish, out_shape=(shape(far_acc.shape, F32), shape(arrive...]
where the time goes in v1:
time: 28.2 us; the launch traced here: 28 us
  Pallas kernels  27.3 us (97%)
  between operations  0.66 us (2%)
    pallas_call x1, Pallas kernels, on_device(): pl.pallas_call(functools.partial(exchange, sizes, capacity), out_shape=(s...  12.1 us
    pallas_call x1, Pallas kernels, on_device(): pl.pallas_call(step_stars, out_shape=shape((6, lanes * capacity * length)...  10.3 us
    pallas_call x1, Pallas kernels, on_device(): pl.pallas_call(functools.partial(deliver, lanes), out_shape=(shape(packed...  4.33 us
    pallas_call x1, Pallas kernels, on_device(): pl.pallas_call(finish, out_shape=(shape(far_acc.shape, F32), shape(arrive...  0.68 us

profile of v1, /device:TPU:0, one launch (start us, length us, event | category | flops | bytes accessed | tf_op | source)
XLA Modules:
  0.0 28.0 jit_solution(10910163091299703845)
XLA Ops:
  0.6 12.1 %exchange.1 = (f32[16,8,128]{2,1,0:T(8,128)S(1)}, s32[24,128]{1,0:T(8,128)S(1)}, f32[4,512]{1,0:T(4,128)S(1)}, bf16[16,512]{1,0:T(8,128)(2,1)S(1)}, f32[32,1,128]{2,1,0:T(1,128)S(1)}) custom-call(f32[3,512]{1,0:T(4,128)} %pos_hbm.1, f32[3,512]{1,0:T(4,128)} %vel_hbm.1, f32[1,512]{1,0:T(1,128)} %bitcast.7, f32[3,512]{1,0:T(4,128)} %far_hbm.1, ...), custom_call_target="tpu_custom_call" | custom-call | tf_op jit(solution)/shard_map/exchange/pallas_call | solution.py:511
  12.7 10.3 %step_stars.1.packed_ref = f32[6,4096]{1,0:T(8,128)S(1)} custom-call(s32[24,128]{1,0:T(8,128)S(1)} %get-tuple-element.9.plan_vmem, f32[16,8,128]{2,1,0:T(8,128)S(1)} %get-tuple-element.10.member_ref), custom_call_target="tpu_custom_call" | custom-call | tf_op jit(solution)/shard_map/step_stars/pallas_call | solution.py:559
  23.0 4.3 %deliver.1 = (f32[6,4096]{1,0:T(8,128)S(1)}, f32[3,512]{1,0:T(4,128)S(1)}) custom-call(f32[6,4096]{1,0:T(8,128)S(1)} %step_stars.1.packed_ref, f32[4,512]{1,0:T(4,128)S(1)} %get-tuple-element.11.star_ref, bf16[16,512]{1,0:T(8,128)(2,1)S(1)} %get-tuple-element.12.right_ref, f32[32,128]{1,0:T(8,128)S(1)} %bitcast.6), custom_call_target="tpu_custom_call" | custom-call | tf_op jit(solution)/shard_map/deliver/pallas_call | solution.py:568
  27.3 0.7 %finish.1 = (f32[3,512]{1,0:T(4,128)}, f32[6,4096]{1,0:T(8,128)}) custom-call(f32[3,512]{1,0:T(4,128)S(1)} %get-tuple-element.14.far_ref, f32[6,4096]{1,0:T(8,128)S(1)} %get-tuple-element.15.arrived_ref), custom_call_target="tpu_custom_call" | custom-call | tf_op jit(solution)/shard_map/finish/pallas_call | solution.py:577

commit v2 on v1

--- a/solution.py
+++ b/solution.py
@@ -136,20 +136,24 @@
         load.start()
     barrier = pltpu.get_barrier_semaphore()
 
-    turned = [[lax.rem(at + k, size) for k in range(size)] for at, size in zip(here[:2], sizes)]
+    outward = here[1] * 2 < sizes[1]
+    steps_y = [jnp.where(outward, sizes[1] - k, k) if k else jnp.int32(0) for k in range(sizes[1])]
+    turned_x = [lax.rem(here[0] + k, sizes[0]) for k in range(sizes[0])]
+    turned_y = [lax.rem(here[1] + k, sizes[1]) for k in steps_y]
     few = sizes[2] <= 4
 
     def each(act):
-        for x, at_x in enumerate(turned[0]):
-            for y, at_y in enumerate(turned[1]):
+        for y in (*range(1, sizes[1]), 0):
+            for x in reversed(range(sizes[0])):
                 first = 1 if x == 0 and y == 0 else 0
 
                 def one(z, carry):
-                    act((x * sizes[1] + y) * sizes[2] + z, (at_x, at_y, lax.rem(here[2] + z, sizes[2])))
+                    slot = (x * sizes[1] + steps_y[y]) * sizes[2] + z
+                    act(slot, (turned_x[x], turned_y[y], lax.rem(here[2] + z, sizes[2])))
                     return carry
 
                 if few:
-                    for z in range(first, sizes[2]):
+                    for z in reversed(range(first, sizes[2])):
                         one(z, 0)
                 else:
                     lax.fori_loop(first, sizes[2], one, 0)
@@ -173,6 +177,41 @@
         sent_ref[number] = found
     every_ref[0] = moments(position, mass, cell_ref[...])
 
+    pl.semaphore_wait(barrier, domains - 1)
+
+    def around(number):
+        offset = (number // 9 - 1, number // 3 % 3 - 1, number % 3 - 1)
+        there = tuple(a + b for a, b in zip(here, offset))
+        inside = functools.reduce(jnp.logical_and, [(a >= 0) & (a < size) for a, size in zip(there, sizes)])
+        return there, inside
+
+    for number in range(27):
+        if number != 13:
+            there, inside = around(number)
+
+            @pl.when(inside)
+            def _():
+                pltpu.make_async_remote_copy(
+                    src_ref=sent_ref,
+                    dst_ref=near_ref.at[26 - number],
+                    send_sem=send_sems.at[number],
+                    recv_sem=recv_sems.at[26 - number],
+                    device_id=there,
+                    device_id_type=MESH,
+                ).start()
+
+    def share(slot, device):
+        pltpu.make_async_remote_copy(
+            src_ref=every_ref.at[0],
+            dst_ref=every_ref.at[slot],
+            send_sem=moment_sems.at[0],
+            recv_sem=moment_sems.at[1],
+            device_id=device,
+            device_id_type=MESH,
+        ).start()
+
+    each(share)
+
     middle = [at.astype(F32) + 0.5 for at in here]
     shift = jnp.where(
         iota((3, stars), 0) == 0, middle[0], jnp.where(iota((3, stars), 0) == 1, middle[1], middle[2])
@@ -202,41 +241,6 @@
                 member_ref[b] = value
 
     gather([(n, lambda piece=piece: piece) for n, piece in enumerate(own)], True)
-    pl.semaphore_wait(barrier, domains - 1)
-
-    def around(number):
-        offset = (number // 9 - 1, number // 3 % 3 - 1, number % 3 - 1)
-        there = tuple(a + b for a, b in zip(here, offset))
-        inside = functools.reduce(jnp.logical_and, [(a >= 0) & (a < size) for a, size in zip(there, sizes)])
-        return there, inside
-
-    for number in range(27):
-        if number != 13:
-            there, inside = around(number)
-
-            @pl.when(inside)
-            def _():
-                pltpu.make_async_remote_copy(
-                    src_ref=sent_ref,
-                    dst_ref=near_ref.at[26 - number],
-                    send_sem=send_sems.at[number],
-                    recv_sem=recv_sems.at[26 - number],
-                    device_id=there,
-                    device_id_type=MESH,
-                ).start()
-
-    def share(slot, device):
-        pltpu.make_async_remote_copy(
-            src_ref=every_ref.at[0],
-            dst_ref=every_ref.at[slot],
-            send_sem=moment_sems.at[0],
-            recv_sem=moment_sems.at[1],
-            device_id=device,
-            device_id_type=MESH,
-        ).start()
-
-    each(share)
-
     def settle(number):
         there, inside = around(number)
 
@@ -267,16 +271,16 @@
                 pieces += reads(slot)
         gather(pieces, False)
 
+    for number in range(27):
+        if number != 13:
+            there, inside = around(number)
+
+            @pl.when(inside)
+            def _():
+                pltpu.make_async_copy(sent_ref, sent_ref, send_sems.at[number]).wait()
     rest = every_ref.at[pl.ds(1, domains - 1)]
     pltpu.make_async_copy(rest, rest, moment_sems.at[0]).wait()
     pltpu.make_async_copy(rest, rest, moment_sems.at[1]).wait()
-    for number in range(27):
-        if number != 13:
-            there, inside = around(number)
-
-            @pl.when(inside)
-            def _():
-                pltpu.make_async_copy(sent_ref, sent_ref, send_sems.at[number]).wait()
 
 
 class Rows:
@@ -337,7 +341,7 @@
 
 
 def step_stars(
-    plan_vmem, member_ref, out_ref, plan_ref, state_ref, force_ref, mass_ref, origin_ref, sem,
+    plan_vmem, member_ref, out_ref, plan_ref, state_ref, force_ref, mass_ref, origin_ref, scale_ref, sem,
 ):
     blocks = member_ref.shape[0]
     fetch = pltpu.make_async_copy(plan_vmem, plan_ref, sem)
@@ -356,6 +360,16 @@
             state_ref[name] = state
             mass_ref[name] = mass
             origin_ref[name] = state - rows.first_used * pltpu.roll(middle, 4, 0) * TIME_STEP
+            count = jnp.broadcast_to(plan_vmem[pl.ds(name, 1), 0:1], (8, LANES)).astype(F32)
+            width = TIME_STEP / jnp.maximum(count, 1.0) * rows.used
+            half, squared = 0.5 * width, width * width
+            for kind, scale in enumerate(
+                (
+                    width, 0.5 * squared, squared * width * (1.0 / 6.0) * rows.first_used, squared * (1.0 / 12.0),
+                    half * rows.last_used, half * rows.first_used,
+                )
+            ):
+                scale_ref[name, kind] = scale
             force_ref[name] = forces(rows, state, mass)
         return carry
 
@@ -365,28 +379,21 @@
     def advance(number, carry):
         step, place = carry
         limit = plan_ref[blocks, step]
-        names, widths = [], []
+        work = []
         for g in range(TOGETHER):
             over = place + g >= limit
             name = jnp.where(over, place + g - limit, place + g)
-            count = plan_ref[name, 0]
-            live = count > step + over.astype(I32)
-            names.append(name)
-            widths.append(jnp.where(live, TIME_STEP / count.astype(F32), 0.0))
+            work.append((name, jnp.where(plan_ref[name, 0] > step + over.astype(I32), 1.0, 0.0)))
         fresh = []
-        for name, width in zip(names, widths):
-            state, force, mass = state_ref[name], force_ref[name], mass_ref[name]
-            h = rows.used * width
-            squared = h * h
-            moving = h * jnp.where(rows.upper, pltpu.roll(state, 4, 0), pltpu.roll(force, 4, 0))
-            cubed = squared * h * (rows.first_used * (1.0 / 6.0))
-            predicted = state + moving + (0.5 * squared) * force + cubed * pltpu.roll(force, 4, 0)
-            force_new = forces(rows, predicted, mass)
+        for name, live in work:
+            state, force = state_ref[name], force_ref[name]
+            moving = scale_ref[name, 0] * jnp.where(rows.upper, pltpu.roll(state, 4, 0), pltpu.roll(force, 4, 0))
+            predicted = state + moving + scale_ref[name, 1] * force + scale_ref[name, 2] * pltpu.roll(force, 4, 0)
+            force_new = forces(rows, predicted, mass_ref[name])
             gap = force - force_new
-            half = 0.5 * h
-            change = moving + squared * (1.0 / 12.0) * gap - half * rows.last_used * pltpu.roll(gap, 4, 0)
-            change = change + half * rows.first_used * pltpu.roll(change, 4, 0)
-            fresh.append((name, state + change, force_new))
+            change = moving + scale_ref[name, 3] * gap - scale_ref[name, 4] * pltpu.roll(gap, 4, 0)
+            change = change + scale_ref[name, 5] * pltpu.roll(change, 4, 0)
+            fresh.append((name, state + live * change, force_new))
         for name, state, force in fresh:
             state_ref[name] = state
             force_ref[name] = force
@@ -561,7 +568,15 @@
         out_shape=shape((6, lanes * capacity * length), F32),
         in_specs=vmem(2),
         out_specs=vmem(1)[0],
-        scratch_shapes=[pltpu.SMEM(plan.shape, I32), block, block, block, block, pltpu.SemaphoreType.DMA],
+        scratch_shapes=[
+            pltpu.SMEM(plan.shape, I32),
+            block,
+            block,
+            block,
+            block,
+            pltpu.VMEM((blocks, 6, 8, LANES), F32),
+            pltpu.SemaphoreType.DMA,
+        ],
         compiler_params=params(),
         name="step_stars",
     )(plan, member)

time: 28.2 us -> 27.3 us (0.968)
  Pallas kernels: 27.3 us -> 26.7 us
    pallas_call x1, Pallas kernels: 10.3 us -> 9.71 us  [on_device(): pl.pallas_call(step_stars, out_shape=shape((6, lanes * capacity * length)...]
where the time goes in v2:
time: 27.3 us; the launch traced here: 27.4 us
  Pallas kernels  26.7 us (98%)
  between operations  0.66 us (2%)
    pallas_call x1, Pallas kernels, on_device(): pl.pallas_call(functools.partial(exchange, sizes, capacity), out_shape=(s...  12 us
    pallas_call x1, Pallas kernels, on_device(): pl.pallas_call(step_stars, out_shape=shape((6, lanes * capacity * length)...  9.71 us
    pallas_call x1, Pallas kernels, on_device(): pl.pallas_call(functools.partial(deliver, lanes), out_shape=(shape(packed...  4.33 us
    pallas_call x1, Pallas kernels, on_device(): pl.pallas_call(finish, out_shape=(shape(far_acc.shape, F32), shape(arrive...  0.68 us

profile of v2, /device:TPU:0, one launch (start us, length us, event | category | flops | bytes accessed | tf_op | source)
XLA Modules:
  0.0 27.4 jit_solution(32629340332816435)
XLA Ops:
  0.6 12.0 %exchange.1 = (f32[16,8,128]{2,1,0:T(8,128)S(1)}, s32[24,128]{1,0:T(8,128)S(1)}, f32[4,512]{1,0:T(4,128)S(1)}, bf16[16,512]{1,0:T(8,128)(2,1)S(1)}, f32[32,1,128]{2,1,0:T(1,128)S(1)}) custom-call(f32[3,512]{1,0:T(4,128)} %pos_hbm.1, f32[3,512]{1,0:T(4,128)} %vel_hbm.1, f32[1,512]{1,0:T(1,128)} %bitcast.7, f32[3,512]{1,0:T(4,128)} %far_hbm.1, ...), custom_call_target="tpu_custom_call" | custom-call | tf_op jit(solution)/shard_map/exchange/pallas_call | solution.py:518
  12.6 9.7 %step_stars.1.packed_ref = f32[6,4096]{1,0:T(8,128)S(1)} custom-call(s32[24,128]{1,0:T(8,128)S(1)} %get-tuple-element.9.plan_vmem, f32[16,8,128]{2,1,0:T(8,128)S(1)} %get-tuple-element.10.member_ref), custom_call_target="tpu_custom_call" | custom-call | tf_op jit(solution)/shard_map/step_stars/pallas_call | solution.py:566
  22.4 4.3 %deliver.1 = (f32[6,4096]{1,0:T(8,128)S(1)}, f32[3,512]{1,0:T(4,128)S(1)}) custom-call(f32[6,4096]{1,0:T(8,128)S(1)} %step_stars.1.packed_ref, f32[4,512]{1,0:T(4,128)S(1)} %get-tuple-element.11.star_ref, bf16[16,512]{1,0:T(8,128)(2,1)S(1)} %get-tuple-element.12.right_ref, f32[32,128]{1,0:T(8,128)S(1)} %bitcast.6), custom_call_target="tpu_custom_call" | custom-call | tf_op jit(solution)/shard_map/deliver/pallas_call | solution.py:583
  26.7 0.7 %finish.1 = (f32[3,512]{1,0:T(4,128)}, f32[6,4096]{1,0:T(8,128)}) custom-call(f32[3,512]{1,0:T(4,128)S(1)} %get-tuple-element.14.far_ref, f32[6,4096]{1,0:T(8,128)S(1)} %get-tuple-element.15.arrived_ref), custom_call_target="tpu_custom_call" | custom-call | tf_op jit(solution)/shard_map/finish/pallas_call | solution.py:592
